TPU v7x, 32 devices: a whole 2x2x4 slice. The times are simulated.
32 devices in a mesh: fsdp: 2 (over x), ctx: 4 (over z), tp: 4 (over y, core).
Axes of the slice: x: 2, y: 2, z: 4, core: 2. Of those that a mesh axis runs over, the one named last changes fastest.
Arguments:
- tokens: bfloat16 [8192, 1024], P(('fsdp', 'ctx')), may hold values from -6 to 6
- w_qkv: bfloat16 [3, 1024, 1024], P(None, 'fsdp', 'tp'), may hold values from -0.25 to 0.25
- w_out: bfloat16 [1024, 1024], P('tp', 'fsdp'), may hold values from -0.75 to 0.75
- w_up: bfloat16 [1024, 4096], P('fsdp', 'tp'), may hold values from -0.1875 to 0.1875
- w_down: bfloat16 [4096, 1024], P('tp', 'fsdp'), may hold values from -0.09375 to 0.09375
- gains: bfloat16 [2, 1024], P(None, 'fsdp'), may hold values from 0.5 to 1.5
- shifts: bfloat16 [2, 1024], P(None, 'fsdp'), may hold values from -3 to 3
- lengths: int32 [2, 3], P('fsdp'), may hold values from 256 to 2048, as said below
- out_grad: bfloat16 [8192, 1024], P(('fsdp', 'ctx')), may hold values from -6 to 6
Outputs:
- out: bfloat16 [8192, 1024], P(('fsdp', 'ctx'))
- input_grad: bfloat16 [8192, 1024], P(('fsdp', 'ctx'))
- grad_qkv: float32 [3, 1024, 1024], P(None, 'fsdp', 'tp')
- grad_out: float32 [1024, 1024], P('tp', 'fsdp')
- grad_up: float32 [1024, 4096], P('fsdp', 'tp')
- grad_down: float32 [4096, 1024], P('tp', 'fsdp')
- grad_gains: float32 [2, 1024], P(None, 'fsdp')
- grad_shifts: float32 [2, 1024], P(None, 'fsdp')
Inputs may be any that keep to these rules, and one draw needn't show every extreme that they name: `lengths`: in each row one sequence has exactly 2048 tokens and the others 2048 // 8 to 1024; sequences lie end to end from the pack's first slot, and the slots after them up to 4096 are padding.
All inputs are finite; a program needn't handle non-finite values.
Results may differ from a plain program's by a relative error of at most 0.014.
The roundings to bfloat16 on the way count: a program that leaves them out, or rounds other values in their place, can miss the bound.
Values may be sent and summed in bfloat16 or wider, within the bound.
No kernel may reach another device: no remote copies, remote signals or barrier semaphores. Data moves between devices by JAX's collectives and lax.ppermute only.
A program may use at most 192 MiB of HBM per device.

v0:
```python
import math
import jax
import jax.numpy as jnp
from jax import lax
from jax.sharding import PartitionSpec as P

HEAD_DIM = 64
SEQS = 3
norm_eps = 1e-12
masked_low = -1e30


def layer_norm(rows, gain, shift):
    centre = rows - jnp.mean(rows, axis=-1, keepdims=True)
    spread = jnp.mean(centre * centre, axis=-1, keepdims=True)
    return centre * lax.rsqrt(spread + norm_eps) * gain + shift


def exact_gelu(values):
    return jax.nn.gelu(values, approximate=False)


def contract_rows(left, right):
    return lax.dot_general(
        left, right, (((0,), (0,)), ((), ())), preferred_element_type=jnp.float32
    )


def contract_cols(left, right):
    return lax.dot_general(
        left, right, (((1,), (1,)), ((), ())), preferred_element_type=jnp.float32
    )


def tp_total(terms):
    return lax.psum(terms, "tp")


def segment_of(lengths_row, total):
    seq_ends = jnp.cumsum(lengths_row)
    positions = jnp.arange(total, dtype=jnp.int32)
    return jnp.sum((positions[:, None] >= seq_ends[None, :]).astype(jnp.int32), axis=1)


def score_block(query_block, seg_block, key_heads, segments):
    raw_scores = jnp.einsum(
        "qhd,khd->hqk", query_block, key_heads, preferred_element_type=jnp.float32
    )
    allowed = (seg_block[:, None] == segments[None, :]) & (segments[None, :] < SEQS)
    return (raw_scores * (1.0 / math.sqrt(HEAD_DIM)), allowed)


def attend_forward(query_heads, seg_mine, key_heads, value_heads, segments):

    def one_block(inputs):
        query_block, seg_block = inputs
        scores, allowed = score_block(query_block, seg_block, key_heads, segments)
        has_key = jnp.any(allowed, axis=1)
        masked = jnp.where(allowed[None], scores, masked_low)
        row_max = jnp.where(has_key[None, :, None], jnp.max(masked, axis=2, keepdims=True), 0.0)
        exp_terms = jnp.where(allowed[None], jnp.exp(masked - row_max), 0.0)
        denominator = (
            jnp.sum(exp_terms, axis=2, keepdims=True)
            + (1.0 - has_key.astype(jnp.float32))[None, :, None]
        )
        attn_probs = (exp_terms / denominator).astype(jnp.bfloat16)
        context = jnp.einsum(
            "hqk,khd->qhd", attn_probs, value_heads, preferred_element_type=jnp.float32
        )
        log_total = row_max[:, :, 0] + jnp.log(denominator[:, :, 0])
        return (context.astype(jnp.bfloat16), log_total)

    return lax.map(one_block, (query_heads, seg_mine))


def attend_backward(
    query_heads, seg_mine, grad_heads, log_totals, key_heads, value_heads, segments
):
    score_scale = 1.0 / math.sqrt(HEAD_DIM)
    zero_keys = jnp.zeros(key_heads.shape, jnp.float32)

    def one_block(carry, inputs):
        key_grad, value_grad = carry
        query_block, seg_block, grad_block, log_block = inputs
        scores, allowed = score_block(query_block, seg_block, key_heads, segments)
        attn_probs = jnp.where(allowed[None], jnp.exp(scores - log_block[:, :, None]), 0.0)
        probs_low = attn_probs.astype(jnp.bfloat16)
        grad_probs = jnp.einsum(
            "qhd,khd->hqk", grad_block, value_heads, preferred_element_type=jnp.float32
        )
        row_delta = jnp.sum(attn_probs * grad_probs, axis=2, keepdims=True)
        grad_scores = (attn_probs * (grad_probs - row_delta) * score_scale).astype(jnp.bfloat16)
        query_grad = jnp.einsum(
            "hqk,khd->qhd", grad_scores, key_heads, preferred_element_type=jnp.float32
        )
        key_grad = key_grad + jnp.einsum(
            "hqk,qhd->khd", grad_scores, query_block, preferred_element_type=jnp.float32
        )
        value_grad = value_grad + jnp.einsum(
            "hqk,qhd->khd", probs_low, grad_block, preferred_element_type=jnp.float32
        )
        return ((key_grad, value_grad), query_grad)

    return lax.scan(
        one_block, (zero_keys, zero_keys), (query_heads, seg_mine, grad_heads, log_totals)
    )


def body(tokens, w_qkv, w_out, w_up, w_down, gains, shifts, lengths, out_grad):
    full_qkv, full_out, full_up, full_down, full_gains, full_shifts = (
        lax.all_gather(w_qkv, "fsdp", axis=1, tiled=True),
        lax.all_gather(w_out, "fsdp", axis=1, tiled=True),
        lax.all_gather(w_up, "fsdp", axis=0, tiled=True),
        lax.all_gather(w_down, "fsdp", axis=1, tiled=True),
        lax.all_gather(gains, "fsdp", axis=1, tiled=True),
        lax.all_gather(shifts, "fsdp", axis=1, tiled=True),
    )
    tok_rows = tokens.shape[0]
    local_width = full_qkv.shape[2]
    local_heads = local_width // HEAD_DIM
    block_rows = min(512, tok_rows)
    block_count = tok_rows // block_rows
    pack_rows = tok_rows * lax.axis_size("ctx")
    segments = segment_of(lengths[0], pack_rows)
    seg_mine = lax.dynamic_slice_in_dim(
        segments, lax.axis_index("ctx") * tok_rows, tok_rows
    ).reshape(block_count, block_rows)
    residual_in = tokens.astype(jnp.float32)
    projected = jnp.einsum(
        "td,sdc->stc", tokens, full_qkv, preferred_element_type=jnp.float32
    ).astype(jnp.bfloat16)
    key_rows, value_rows = (
        lax.all_gather(projected[1], "ctx", axis=0, tiled=True),
        lax.all_gather(projected[2], "ctx", axis=0, tiled=True),
    )
    key_heads = key_rows.reshape(pack_rows, local_heads, HEAD_DIM)
    value_heads = value_rows.reshape(pack_rows, local_heads, HEAD_DIM)
    query_heads = projected[0].reshape(block_count, block_rows, local_heads, HEAD_DIM)
    context_blocks, log_totals = attend_forward(
        query_heads, seg_mine, key_heads, value_heads, segments
    )
    context = context_blocks.reshape(tok_rows, local_width)
    attn_terms = jnp.dot(context, full_out, preferred_element_type=jnp.float32)
    resid_rows = residual_in + tp_total(attn_terms)
    grad_rows = out_grad.astype(jnp.float32)
    gain_full = full_gains.astype(jnp.float32)
    shift_full = full_shifts.astype(jnp.float32)
    hidden, norm_first = jax.vjp(layer_norm, resid_rows, gain_full[0], shift_full[0])
    hidden_part = hidden.astype(jnp.bfloat16)
    pre_act = jnp.dot(hidden_part, full_up, preferred_element_type=jnp.float32)
    activated, gelu_back = jax.vjp(exact_gelu, pre_act)
    act_low = activated.astype(jnp.bfloat16)
    ffn_terms = jnp.dot(act_low, full_down, preferred_element_type=jnp.float32)
    ffn_rows = tp_total(ffn_terms)
    result, norm_second = jax.vjp(layer_norm, hidden + ffn_rows, gain_full[1], shift_full[1])
    grad_mid, gain_second, shift_second = norm_second(grad_rows)
    mid_part = grad_mid.astype(jnp.bfloat16)
    result_part = result.astype(jnp.bfloat16)
    back_qkv, back_out, back_up, back_down = (
        lax.all_gather(w_qkv, "fsdp", axis=1, tiled=True),
        lax.all_gather(w_out, "fsdp", axis=1, tiled=True),
        lax.all_gather(w_up, "fsdp", axis=0, tiled=True),
        lax.all_gather(w_down, "fsdp", axis=1, tiled=True),
    )
    down_grad = contract_rows(act_low, mid_part)
    act_grad = contract_cols(mid_part, back_down)
    (pre_grad,) = gelu_back(act_grad)
    pre_low = pre_grad.astype(jnp.bfloat16)
    up_grad = contract_rows(hidden_part, pre_low)
    hidden_terms = contract_cols(pre_low, back_up)
    hidden_grad = grad_mid + tp_total(hidden_terms)
    resid_grad, gain_first, shift_first = norm_first(hidden_grad)
    attn_part = resid_grad.astype(jnp.bfloat16)
    out_proj_grad = contract_rows(context, attn_part)
    context_grad = contract_cols(attn_part, back_out).astype(jnp.bfloat16)
    grad_heads = context_grad.reshape(block_count, block_rows, local_heads, HEAD_DIM)
    (key_grad, value_grad), query_grad = attend_backward(
        query_heads, seg_mine, grad_heads, log_totals, key_heads, value_heads, segments
    )
    key_mine, value_mine = (
        lax.psum_scatter(
            key_grad.reshape(pack_rows, local_width), "ctx", scatter_dimension=0, tiled=True
        ),
        lax.psum_scatter(
            value_grad.reshape(pack_rows, local_width), "ctx", scatter_dimension=0, tiled=True
        ),
    )
    proj_grad = jnp.stack(
        [
            query_grad.reshape(tok_rows, local_width).astype(jnp.bfloat16),
            key_mine.astype(jnp.bfloat16),
            value_mine.astype(jnp.bfloat16),
        ]
    )
    qkv_grad = jnp.einsum("td,stc->sdc", tokens, proj_grad, preferred_element_type=jnp.float32)
    input_part = jnp.einsum("stc,sdc->td", proj_grad, back_qkv, preferred_element_type=jnp.float32)
    input_grad = (resid_grad + tp_total(input_part)).astype(jnp.bfloat16)
    gain_grad = jnp.stack([gain_first, gain_second])
    shift_grad = jnp.stack([shift_first, shift_second])
    qkv_grad, out_proj_grad, up_grad, down_grad, gain_grad, shift_grad = (
        lax.psum_scatter(qkv_grad, "fsdp", scatter_dimension=1, tiled=True),
        lax.psum_scatter(out_proj_grad, "fsdp", scatter_dimension=1, tiled=True),
        lax.psum_scatter(up_grad, "fsdp", scatter_dimension=0, tiled=True),
        lax.psum_scatter(down_grad, "fsdp", scatter_dimension=1, tiled=True),
        lax.psum_scatter(gain_grad, "fsdp", scatter_dimension=1, tiled=True),
        lax.psum_scatter(shift_grad, "fsdp", scatter_dimension=1, tiled=True),
    )
    qkv_grad, out_proj_grad, up_grad, down_grad, gain_grad, shift_grad = lax.psum(
        (qkv_grad, out_proj_grad, up_grad, down_grad, gain_grad, shift_grad), "ctx"
    )
    return (
        result_part,
        input_grad,
        qkv_grad,
        out_proj_grad,
        up_grad,
        down_grad,
        gain_grad,
        shift_grad,
    )


def solution(mesh):
    return jax.shard_map(
        body,
        mesh=mesh,
        in_specs=(
            P(("fsdp", "ctx"), None),
            P(None, "fsdp", "tp"),
            P("tp", "fsdp"),
            P("fsdp", "tp"),
            P("tp", "fsdp"),
            P(None, "fsdp"),
            P(None, "fsdp"),
            P("fsdp", None),
            P(("fsdp", "ctx"), None),
        ),
        out_specs=(
            P(("fsdp", "ctx"), None),
            P(("fsdp", "ctx"), None),
            P(None, "fsdp", "tp"),
            P("tp", "fsdp"),
            P("fsdp", "tp"),
            P("tp", "fsdp"),
            P(None, "fsdp"),
            P(None, "fsdp"),
        ),
        check_vma=False,
    )
```

profile of v0, /device:TPU:0, one launch (start us, length us, event | category | flops | bytes accessed | tf_op | source)
XLA Modules:
  0.0 1667.1 jit_solution(5852999273512513464)
XLA Ops:
  9.6 30.5 %all-gather.8.cloned.1.call-done = bf16[3,1024,256]{1,2,0:T(8,128)(2,1)} async-done(((bf16[3,512,256]{1,2,0:T(8,128)(2,1)}), bf16[3,1024,256]{1,2,0:T(8,128)(2,1)}) %all-gather.8.cloned.1.call-update) | async-done | bytes 1572880 | tf_op jit(solution)/shard_map/all_gather | solution.py:111
  40.1 3.9 fusion.111
  46.3 9.0 all_gather.31
  55.7 35.5 %all-gather.14.cloned.1.call-done = bf16[1,4096,256]{1,2,0:T(8,128)(2,1)} async-done(((bf16[1,1024,256]{1,2,0:T(8,128)(2,1)}), bf16[1,4096,256]{1,2,0:T(8,128)(2,1)}) %all-gather.14.cloned.1.call-update) | async-done | bytes 2097168 | tf_op jit(solution)/shard_map/all_gather | solution.py:133
  91.2 46.9 %all-gather.16.cloned.1.call-done = bf16[1,4096,256]{1,2,0:T(8,128)(2,1)} async-done(((bf16[1,1024,256]{1,2,0:T(8,128)(2,1)}), bf16[1,4096,256]{1,2,0:T(8,128)(2,1)}) %all-gather.16.cloned.1.call-update) | async-done | bytes 2097168 | tf_op jit(solution)/shard_map/all_gather | solution.py:134
  138.0 99.9 %while.27 = (s32[]{:T(128)}, bf16[2,512,4,64]{1,3,2,0:T(8,128)(2,1)}, f32[2,4,512]{2,1,0:T(4,128)S(1)}, s32[2,512]{1,0:T(2,128)S(1)}, s32[4096]{0:T(1024)S(1)}, ...) while((s32[]{:T(128)}, ...), condition=%wide.region_6.7_spmd, body=%wide.region_2.6_spmd.sunk | while | flops 2271357440 | bytes 113924704 | solution.py:73
  140.3 15.8 fusion.181
  156.1 15.6 fusion.182
  171.8 16.2 fusion.183
  190.3 15.8 fusion.181
  206.1 15.6 fusion.182
  221.7 16.2 fusion.183
  240.4 2.7 fusion.134
  244.4 4.3 all_gather.32
  248.7 4.6 all_gather.33
  253.3 74.2 %all-reduce.8.cloned.1.call-done = f32[1024,1024]{1,0:T(8,128)} async-done(((f32[1024,1024]{1,0:T(8,128)}), f32[1024,1024]{1,0:T(8,128)}) %all-reduce.8.cloned.1.call-update) | async-done | bytes 4194320 | tf_op jit(solution)/shard_map/psum | solution.py:36
  327.5 2.7 fusion.130
  332.7 29.5 %all-gather.10.cloned.1.call-done = bf16[1024,1024]{1,0:T(8,128)(2,1)} async-done(((bf16[512,1024]{1,0:T(8,128)(2,1)}), bf16[1024,1024]{1,0:T(8,128)(2,1)}) %all-gather.10.cloned.1.call-update) | async-done | bytes 2097168 | tf_op jit(solution)/shard_map/all_gather | solution.py:113
  362.2 15.5 multiply_convert_fusion.1
  377.7 19.1 %all-gather.12.cloned.1.call-done = bf16[1024,1024]{1,0:T(8,128)(2,1)} async-done(((bf16[1024,512]{1,0:T(8,128)(2,1)}), bf16[1024,1024]{1,0:T(8,128)(2,1)}) %all-gather.12.cloned.1.call-update) | async-done | bytes 2097168 | tf_op jit(solution)/shard_map/all_gather | solution.py:114
  396.9 6.5 fusion.135
  403.8 85.2 %all-reduce.10.cloned.1.call-done = f32[1024,1024]{1,0:T(8,128)} async-done(((f32[1024,1024]{1,0:T(8,128)}), f32[1024,1024]{1,0:T(8,128)}) %all-reduce.10.cloned.1.call-update) | async-done | bytes 4194320 | tf_op jit(solution)/shard_map/psum | solution.py:36
  489.0 4.2 fusion.127
  497.5 3.2 fusion.126
  500.6 3.1 copy-done.39
  503.7 3.9 add_convert_fusion.1
  509.0 4.3 fusion.136
  513.4 85.7 %all-reduce.12.cloned.1.call-done = f32[1024,1024]{1,0:T(8,128)} async-done(((f32[1024,1024]{1,0:T(8,128)}), f32[1024,1024]{1,0:T(8,128)}) %all-reduce.12.cloned.1.call-update) | async-done | bytes 4194320 | tf_op jit(solution)/shard_map/psum | solution.py:36
  599.1 6.4 multiply_reduce_fusion.1
  610.8 2.8 reshape.357
  615.2 341.7 %while.28 = (s32[]{:T(128)}, f32[4096,4,64]{0,2,1:T(8,128)}, f32[4096,4,64]{0,2,1:T(8,128)}, bf16[2,512,4,64]{1,3,2,0:T(8,128)(2,1)}, bf16[2,512,4,64]{1,3,2,0:T...) while((s32[]{:T(128)}, f32[4096,4,64]{0,2,1:T(8,128)}, ...), condition=%wide.region_20.21_spmd.clone, body=%wide.region_18.20_spmd.clone.sunk | while | flops 5595217920 | bytes 414817440 | solution.py:104
  615.4 2.8 compare_and_fusion.3
  618.2 13.1 fusion.196
  631.3 13.1 fusion.195
  644.4 63.5 %fusion.197 = f32[4096,4,64]{0,2,1:T(8,128)} fusion(f32[4,512,4096]{2,1,0:T(8,128)} %fusion.195, f32[4,512,4096]{2,1,0:T(8,128)} %fusion.196, f32[4,512]{1,0:T(4,128)S(1)} %dynamic-slice_bitcast_fusion.2, pred[512,4096]{1,0:T(8,128)(4,1)} %compare_and_fusion.3, f32[4096,4,64]{0,2,1:T(8,128)} %get-tuple-element.498, pred[]{:T(512)S(6)} %compare.3, ...), kind=kOutput, calls=%fused_computation.48.clone.1 | convolution fusion | flops 1168119808 | bytes 147079680 | tf_op jit(solution)/shard_map/while/body/eval_jaxpr/hqk,qhd->khd/dot_general | solution.py:96
  708.0 60.0 %fusion.199 = bf16[2,512,4,64]{1,3,2,0:T(8,128)(2,1)} fusion(bf16[2,512,4,64]{1,3,2,0:T(8,128)(2,1)} %get-tuple-element.500, s32[]{:T(128)} %get-tuple-element.497, bf16[4096,4,64]{0,2,1:T(8,128)(2,1)S(1)} %get-tuple-element.517, f32[4,512,4096]{2,1,0:T(8,128)} %fusion.195, f32[4,512,4096]{2,1,0:T(8,128)} %fusion.196, ...), kind=kOutput, calls=%fused_computation.52.clone.1 | convolution fusion | flops 1166022656 | bytes 141050368 | tf_op jit(solution)/shard_map/while/body/eval_jaxpr/hqk,khd->qhd/dot_general | solution.py:93
  767.9 17.3 %fusion.198 = f32[4096,4,64]{0,2,1:T(8,128)} fusion(f32[4,512,4096]{2,1,0:T(8,128)} %fusion.196, f32[4,512]{1,0:T(4,128)S(1)} %dynamic-slice_bitcast_fusion.2, pred[512,4096]{1,0:T(8,128)(4,1)} %compare_and_fusion.3, f32[4096,4,64]{0,2,1:T(8,128)} %get-tuple-element.499, pred[]{:T(512)S(6)} %compare.3, ...), kind=kOutput, calls=%fused_computation.50.clone.1 | convolution fusion | flops 1109393408 | bytes 44310532 | tf_op jit(solution)/shard_map/while/body/eval_jaxpr/hqk,qhd->khd/dot_general | solution.py:99
  785.2 2.8 compare_and_fusion.3
  788.1 13.1 fusion.196
  801.2 13.1 fusion.195
  814.3 64.0 %fusion.197 = f32[4096,4,64]{0,2,1:T(8,128)} fusion(f32[4,512,4096]{2,1,0:T(8,128)} %fusion.195, f32[4,512,4096]{2,1,0:T(8,128)} %fusion.196, f32[4,512]{1,0:T(4,128)S(1)} %dynamic-slice_bitcast_fusion.2, pred[512,4096]{1,0:T(8,128)(4,1)} %compare_and_fusion.3, f32[4096,4,64]{0,2,1:T(8,128)} %get-tuple-element.498, pred[]{:T(512)S(6)} %compare.3, ...), kind=kOutput, calls=%fused_computation.48.clone.1 | convolution fusion | flops 1168119808 | bytes 147079680 | tf_op jit(solution)/shard_map/while/body/eval_jaxpr/hqk,qhd->khd/dot_general | solution.py:96
  878.3 60.0 %fusion.199 = bf16[2,512,4,64]{1,3,2,0:T(8,128)(2,1)} fusion(bf16[2,512,4,64]{1,3,2,0:T(8,128)(2,1)} %get-tuple-element.500, s32[]{:T(128)} %get-tuple-element.497, bf16[4096,4,64]{0,2,1:T(8,128)(2,1)S(1)} %get-tuple-element.517, f32[4,512,4096]{2,1,0:T(8,128)} %fusion.195, f32[4,512,4096]{2,1,0:T(8,128)} %fusion.196, ...), kind=kOutput, calls=%fused_computation.52.clone.1 | convolution fusion | flops 1166022656 | bytes 141050368 | tf_op jit(solution)/shard_map/while/body/eval_jaxpr/hqk,khd->qhd/dot_general | solution.py:93
  938.3 18.5 %fusion.198 = f32[4096,4,64]{0,2,1:T(8,128)} fusion(f32[4,512,4096]{2,1,0:T(8,128)} %fusion.196, f32[4,512]{1,0:T(4,128)S(1)} %dynamic-slice_bitcast_fusion.2, pred[512,4096]{1,0:T(8,128)(4,1)} %compare_and_fusion.3, f32[4096,4,64]{0,2,1:T(8,128)} %get-tuple-element.499, pred[]{:T(512)S(6)} %compare.3, ...), kind=kOutput, calls=%fused_computation.50.clone.1 | convolution fusion | flops 1109393408 | bytes 44310532 | tf_op jit(solution)/shard_map/while/body/eval_jaxpr/hqk,qhd->khd/dot_general | solution.py:99
  956.9 5.6 copy.61
  962.7 5.6 copy.60
  969.5 4.1 fusion.120
  973.7 6.6 fusion.118
  981.9 6.7 fusion.121
  992.0 47.7 %reduce-scatter.15.cloned.1.call-done = f32[1024,256]{1,0:T(8,128)} async-done(((f32[4096,256]{1,0:T(8,128)}), f32[1024,256]{1,0:T(8,128)}) %reduce-scatter.15.cloned.1.call-update) | async-done | bytes 1048592 | tf_op jit(solution)/shard_map/reduce_scatter | solution.py:184
  1040.9 78.2 %reduce-scatter.13.cloned.1.call-done = f32[1024,256]{1,0:T(8,128)} async-done(((f32[4096,256]{1,0:T(8,128)}), f32[1024,256]{1,0:T(8,128)}) %reduce-scatter.13.cloned.1.call-update) | async-done | bytes 1048592 | tf_op jit(solution)/shard_map/reduce_scatter | solution.py:181
  1121.2 4.5 fusion.105
  1128.1 5.3 convolution_bitcast_fusion
  1133.5 9.4 reduce-scatter.19.cloned.1.call-done
  1142.9 56.5 %reduce-scatter.23.cloned.1.call-done = f32[1024,512]{1,0:T(8,128)} async-done(((f32[1024,1024]{1,0:T(8,128)}), f32[1024,512]{1,0:T(8,128)}) %reduce-scatter.23.cloned.1.call-update) | async-done | bytes 2097168 | tf_op jit(solution)/shard_map/reduce_scatter | solution.py:204
  1199.4 56.7 %reduce-scatter.21.cloned.1.call-done = f32[512,1024]{1,0:T(8,128)} async-done(((f32[1024,1024]{1,0:T(8,128)}), f32[512,1024]{1,0:T(8,128)}) %reduce-scatter.21.cloned.1.call-update) | async-done | bytes 2097168 | tf_op jit(solution)/shard_map/reduce_scatter | solution.py:203
  1256.1 45.5 %reduce-scatter.17.cloned.1.call-done = f32[3,512,256]{1,2,0:T(8,128)} async-done(((f32[3,1024,256]{1,2,0:T(8,128)}), f32[3,512,256]{1,2,0:T(8,128)}) %reduce-scatter.17.cloned.1.call-update) | async-done | bytes 1572880 | tf_op jit(solution)/shard_map/reduce_scatter | solution.py:201
  1301.6 17.3 %reduce-scatter.25.cloned.1.call-done = f32[512,2]{1,0:T(8,128)} async-done(((f32[1024,2]{1,0:T(8,128)}), f32[512,2]{1,0:T(8,128)}) %reduce-scatter.25.cloned.1.call-update) | async-done | bytes 4112
  1320.0 16.2 reduce-scatter.27.cloned.1.call-done
  1337.2 12.4 all-reduce
  1349.7 74.4 %all-reduce.14.cloned.1.call-done = f32[1024,1024]{1,0:T(8,128)} async-done(((f32[1024,1024]{1,0:T(8,128)}), f32[1024,1024]{1,0:T(8,128)}) %all-reduce.14.cloned.1.call-update) | async-done | bytes 4194320 | tf_op jit(solution)/shard_map/psum | solution.py:36
  1424.0 5.2 add_convert_fusion
  1429.2 221.3 %all-reduce.16.cloned.1.call-done = (f32[3,512,256]{1,2,0:T(8,128)}, f32[256,512]{1,0:T(8,128)}, f32[512,1024]{1,0:T(8,128)}, f32[1024,512]{1,0:T(8,128)}) async-done(((f32[3,512,256]{1,2,0:T(8,128)}, f32[256,512]{1,0:T(8,128)}, f32[512,1024]{1,0:T(8,128)}, f32[1024,512]{1,0:T(8,128)}), (f32[3,512,256]{1,2,0:T(8,128)}, f32[256,512]{1,0:T(8,128)}, f32[512,1024]{1,0:T(8,128)}, ...) | async-done | bytes 6291472 | tf_op jit(solution)/shard_map/psum | solution.py:208
  1650.5 3.2 copy.65
  1655.6 3.2 copy.110
  (186 shorter events, 46.0 us)
Async XLA Ops:
  7.2 32.9 %all-gather.8.cloned.1.call-start = ((), (), s32[]{:S(2)}) async-start(), calls=%async_computation.8 | async-start | bytes 2359296 | tf_op jit(solution)/shard_map/all_gather | solution.py:111
  9.5 81.6 %all-gather.14.cloned.1.call-start = ((), (), s32[]{:S(2)}) async-start(), calls=%async_computation.21 | async-start | bytes 2621440 | tf_op jit(solution)/shard_map/all_gather | solution.py:133
  44.0 1.9 copy-start.37
  44.0 2.3 copy-start.16
  45.1 92.9 %all-gather.16.cloned.1.call-start = ((), (), s32[]{:S(2)}) async-start(), calls=%async_computation.22 | async-start | bytes 2621440 | tf_op jit(solution)/shard_map/all_gather | solution.py:134
  45.8 281.7 %all-reduce.8.cloned.1.call-start = ((), (), s32[]{:S(2)}) async-start(), calls=%async_computation.9 | async-start | bytes 8388608 | tf_op jit(solution)/shard_map/psum | solution.py:36
  138.0 102.4 %copy-start.11 = (bf16[256,1024]{1,0:T(8,128)(2,1)S(1)}, bf16[256,1024]{1,0:T(8,128)(2,1)}, u32[]{:S(2)}) copy-start(bf16[256,1024]{1,0:T(8,128)(2,1)} %all_gather.31) | copy-start | bytes 1572868
  239.6 0.8 copy-start.7
  243.1 1.2 copy-start.33
  243.1 5.6 copy-start.34
  243.1 84.4 %copy-start.9 = (bf16[1024,1024]{1,0:T(8,128)(2,1)S(1)}, bf16[1024,1024]{1,0:T(8,128)(2,1)}, u32[]{:S(2)}) copy-start(bf16[1024,1024]{1,0:T(8,128)(2,1)} %param.13) | copy-start | bytes 6291460
  243.2 119.1 %all-gather.10.cloned.1.call-start = ((), (), s32[]{:S(2)}) async-start(), calls=%async_computation.10 | async-start | bytes 3145728 | tf_op jit(solution)/shard_map/all_gather | solution.py:113
  243.7 153.1 %all-gather.12.cloned.1.call-start = ((), (), s32[]{:S(2)}) async-start(), calls=%async_computation.11 | async-start | bytes 3145728 | tf_op jit(solution)/shard_map/all_gather | solution.py:114
  244.3 244.7 %all-reduce.10.cloned.1.call-start = ((), (), s32[]{:S(2)}) async-start(), calls=%async_computation.12 | async-start | bytes 8388608 | tf_op jit(solution)/shard_map/psum | solution.py:36
  248.7 356.8 %copy-start.21 = (f32[1,1024]{1,0:T(1,128)}, f32[1,1024]{1,0:T(1,128)S(1)}, u32[]{:S(2)}) copy-start(f32[1,1024]{1,0:T(1,128)S(1)} %get-tuple-element.329) | copy-start | bytes 12292
  253.3 235.7 %copy-start.28 = (f32[1,1024]{1,0:T(1,128)}, f32[1,1024]{1,0:T(1,128)S(1)}, u32[]{:S(2)}) copy-start(f32[1,1024]{1,0:T(1,128)S(1)} %get-tuple-element.331) | copy-start | bytes 12292
  330.2 2.0 copy-start
  330.2 275.3 %copy-start.17 = (f32[1024]{0:T(1024)}, f32[1024]{0:T(1024)S(1)}, u32[]{:S(2)}) copy-start(f32[1024]{0:T(1024)S(1)} %broadcast_multiply_fusion.1) | copy-start | bytes 12292
  332.7 272.8 %copy-start.19 = (f32[1024]{0:T(1024)}, f32[1024]{0:T(1024)S(1)}, u32[]{:S(2)}) copy-start(f32[1024]{0:T(1024)S(1)} %fusion.114) | copy-start | bytes 12292
  403.4 195.7 %all-reduce.12.cloned.1.call-start = ((), (), s32[]{:S(2)}) async-start(), calls=%async_computation.13 | async-start | bytes 8388608 | tf_op jit(solution)/shard_map/psum | solution.py:36
  493.3 1.6 copy-start.6
  497.4 3.2 copy-start.36
  497.4 3.2 copy-start.38
  497.4 6.3 copy-start.39
  500.6 7.0 copy-start.5
  500.6 98.5 %copy-start.25 = (f32[1024]{0:T(1024)}, f32[1024]{0:T(1024)S(1)}, u32[]{:S(2)}) copy-start(f32[1024]{0:T(1024)S(1)} %negate_multiply_fusion.2) | copy-start | bytes 12292
  503.7 5.2 copy-start.35
  507.6 1.3 copy-start.41
  513.3 526.3 %reduce-scatter.15.cloned.1.call-start = ((), (), s32[]{:S(2)}) async-start(), calls=%async_computation.15 | async-start | bytes 5242880 | tf_op jit(solution)/shard_map/reduce_scatter | solution.py:184
  599.1 6.4 copy-start.1
  607.2 2.0 copy-start.4
  607.3 7.9 copy-start.23
  609.2 5.9 copy-start.2
  618.2 13.1 copy-start.3
  788.1 13.1 copy-start.3
  962.6 156.5 %reduce-scatter.13.cloned.1.call-start = ((), (), s32[]{:S(2)}) async-start(), calls=%async_computation.14 | async-start | bytes 5242880 | tf_op jit(solution)/shard_map/reduce_scatter | solution.py:181
  968.3 1.2 copy-start.8
  968.3 1.2 copy-start.24
  968.3 5.4 copy-start.26
  968.3 5.4 copy-start.40
  968.3 174.5 %reduce-scatter.19.cloned.1.call-start = ((), (), s32[]{:S(2)}) async-start(), calls=%async_computation.18 | async-start | bytes 1572864 | tf_op jit(solution)/shard_map/reduce_scatter | solution.py:202
  973.6 225.7 %reduce-scatter.23.cloned.1.call-start = ((), (), s32[]{:S(2)}) async-start(), calls=%async_computation.20 | async-start | bytes 6291456 | tf_op jit(solution)/shard_map/reduce_scatter | solution.py:204
  980.3 0.7 copy-start.18
  980.3 0.7 copy-start.20
  980.3 0.7 copy-start.22
  980.3 0.7 copy-start.29
  980.3 1.6 copy-start.42
  980.4 275.7 %reduce-scatter.21.cloned.1.call-start = ((), (), s32[]{:S(2)}) async-start(), calls=%async_computation.19 | async-start | bytes 6291456 | tf_op jit(solution)/shard_map/reduce_scatter | solution.py:203
  988.7 132.5 %copy-start.10 = (bf16[1024,1024]{1,0:T(8,128)(2,1)S(1)}, bf16[1024,1024]{1,0:T(8,128)(2,1)}, u32[]{:S(2)}) copy-start(bf16[1024,1024]{1,0:T(8,128)(2,1)} %param.13) | copy-start | bytes 6291460
  988.7 312.8 %reduce-scatter.17.cloned.1.call-start = ((), (), s32[]{:S(2)}) async-start(), calls=%async_computation.17 | async-start | bytes 4718592 | tf_op jit(solution)/shard_map/reduce_scatter | solution.py:201
  1120.4 0.8 copy-start.14
  1121.2 4.6 copy-start.30
  1121.2 4.6 copy-start.32
  1125.7 1.2 copy-start.27
  1125.7 1.2 copy-start.31
  1125.7 2.4 copy-start.13
  1125.7 2.4 copy-start.15
  1125.8 193.1 %reduce-scatter.25.cloned.1.call-start = ((), (), s32[]{:S(2)}) async-start(), calls=%async_computation.23 | async-start | bytes 786432
  1126.9 209.2 %reduce-scatter.27.cloned.1.call-start = ((), (), s32[]{:S(2)}) async-start(), calls=%async_computation.24 | async-start | bytes 786432
  1128.0 296.0 %all-reduce.14.cloned.1.call-start = ((), (), s32[]{:S(2)}) async-start(), calls=%async_computation.16 | async-start | bytes 8388608 | tf_op jit(solution)/shard_map/psum | solution.py:36
  1133.4 517.1 %all-reduce.16.cloned.1.call-start = ((), (), s32[]{:S(2)}) async-start(), calls=%async_computation.25 | async-start | bytes 12582912 | tf_op jit(solution)/shard_map/psum | solution.py:208
  1650.5 8.2 copy-start.12
Sparse Core Ops, SparseCore 0:
  10.1 29.8 all-gather.7
  45.2 45.9 all-gather.13
  93.3 44.6 all-gather.15
  243.3 84.1 all-reduce.7
  329.0 33.2 all-gather.9
  363.7 33.1 all-gather.11
  403.5 85.4 all-reduce.9
  513.5 85.6 all-reduce.11
  962.7 76.8 reduce-scatter.14
  1041.8 77.2 reduce-scatter.12
  1122.0 20.8 reduce-scatter.18
  1145.0 54.3 reduce-scatter.22
  1201.8 54.2 reduce-scatter.20
  1258.2 43.3 reduce-scatter.16
  1304.3 14.5 reduce-scatter.24
  1321.6 14.5 reduce-scatter.26
  1338.5 85.4 all-reduce.13
  1426.5 223.9 all-reduce.15
where the time goes:
time: 1670 us
  waiting for transfers between devices  1030 us (62%)
  matrix products  465 us (28%)
  other arithmetic  71.4 us (4%)
  local copies, waits for them, and re-layouts  51.7 us (3%)
  blocking collectives  30.3 us (2%)
    psum x4, waiting for transfers between devices, tp_total(): return lax.psum(terms, 'tp')  319 us
    psum x1, waiting for transfers between devices, body(): lax.psum((qkv_grad, out_proj_grad, up_grad, down_grad, gain_grad, shift_g...  221 us
    dot_general x2, matrix products, one_block(): jnp.einsum('hqk,qhd->khd', grad_scores, query_block, preferred_element_ty...  128 us
    dot_general x2, matrix products, one_block(): jnp.einsum('hqk,khd->qhd', grad_scores, key_heads, preferred_element_type...  120 us
    reduce_scatter x1, waiting for transfers between devices, body(): lax.psum_scatter(key_grad.reshape(pack_rows, local_width), 'ctx', scatter...  78.2 us
    dot_general x4, matrix products, score_block(): jnp.einsum('qhd,khd->hqk', query_block, key_heads, preferred_element_type...  57.8 us
    reduce_scatter x1, waiting for transfers between devices, body(): lax.psum_scatter(up_grad, 'fsdp', scatter_dimension=0, tiled=True)  56.7 us
    reduce_scatter x1, waiting for transfers between devices, body(): lax.psum_scatter(down_grad, 'fsdp', scatter_dimension=1, tiled=True)  56.5 us
  transfers between devices with their start and end apart: 18, of which 18 were waited for; matrix products, arithmetic and copies ran while one was open for 4% of the time, Pallas kernels for 0%

commit v1 on v0

--- a/solution.py
+++ b/solution.py
@@ -33,7 +33,7 @@
 
 
 def tp_total(terms):
-    return lax.psum(terms, "tp")
+    return jnp.sum(lax.all_gather(terms, "tp"), axis=0)
 
 
 def segment_of(lengths_row, total):

time: 1670 us -> 1780 us (1.066)
  waiting for transfers between devices: 1030 us -> 1100 us
  other arithmetic: 71.4 us -> 113 us
    all_gather x0 -> x4, waiting for transfers between devices: none -> 410 us  [tp_total(): return jnp.sum(lax.all_gather(terms, 'tp'), axis=0)]
    psum x4 -> x0, waiting for transfers between devices: 319 us -> none  [tp_total(): return lax.psum(terms, 'tp')]
    reduce_sum x0 -> x4, other arithmetic: none -> 41.4 us  [tp_total(): return jnp.sum(lax.all_gather(terms, 'tp'), axis=0)]
where the time goes in v1:
time: 1780 us; the launch traced here: 1770 us
  waiting for transfers between devices  1100 us (62%)
  matrix products  462 us (26%)
  other arithmetic  113 us (6%)
  local copies, waits for them, and re-layouts  50.6 us (3%)
  blocking collectives  31 us (2%)
    all_gather x4, waiting for transfers between devices, tp_total(): return jnp.sum(lax.all_gather(terms, 'tp'), axis=0)  410 us
    psum x1, waiting for transfers between devices, body(): lax.psum((qkv_grad, out_proj_grad, up_grad, down_grad, gain_grad, shift_g...  213 us
    dot_general x2, matrix products, one_block(): jnp.einsum('hqk,qhd->khd', grad_scores, query_block, preferred_element_ty...  126 us
    dot_general x2, matrix products, one_block(): jnp.einsum('hqk,khd->qhd', grad_scores, key_heads, preferred_element_type...  118 us
    reduce_scatter x1, waiting for transfers between devices, body(): lax.psum_scatter(key_grad.reshape(pack_rows, local_width), 'ctx', scatter...  78.3 us
    dot_general x4, matrix products, score_block(): jnp.einsum('qhd,khd->hqk', query_block, key_heads, preferred_element_type...  57.9 us
    reduce_scatter x1, waiting for transfers between devices, body(): lax.psum_scatter(up_grad, 'fsdp', scatter_dimension=0, tiled=True)  56.6 us
    reduce_scatter x1, waiting for transfers between devices, body(): lax.psum_scatter(down_grad, 'fsdp', scatter_dimension=1, tiled=True)  48.1 us
  transfers between devices with their start and end apart: 18, of which 18 were waited for; matrix products, arithmetic and copies ran while one was open for 4% of the time, Pallas kernels for 0%

profile of v1, /device:TPU:0, one launch (start us, length us, event | category | flops | bytes accessed | tf_op | source)
XLA Modules:
  0.0 1773.4 jit_solution(15968648537390891308)
XLA Ops:
  9.6 30.5 %all-gather.16.cloned.1.call-done = bf16[3,1024,256]{1,2,0:T(8,128)(2,1)} async-done(((bf16[3,512,256]{1,2,0:T(8,128)(2,1)}), bf16[3,1024,256]{1,2,0:T(8,128)(2,1)}) %all-gather.16.cloned.1.call-update) | async-done | bytes 1572880 | tf_op jit(solution)/shard_map/all_gather | solution.py:111
  40.1 3.9 fusion.111
  46.3 9.4 all_gather.55
  56.1 35.1 %all-gather.22.cloned.1.call-done = bf16[1,4096,256]{1,2,0:T(8,128)(2,1)} async-done(((bf16[1,1024,256]{1,2,0:T(8,128)(2,1)}), bf16[1,4096,256]{1,2,0:T(8,128)(2,1)}) %all-gather.22.cloned.1.call-update) | async-done | bytes 2097168 | tf_op jit(solution)/shard_map/all_gather | solution.py:133
  91.2 46.9 %all-gather.24.cloned.1.call-done = bf16[1,4096,256]{1,2,0:T(8,128)(2,1)} async-done(((bf16[1,1024,256]{1,2,0:T(8,128)(2,1)}), bf16[1,4096,256]{1,2,0:T(8,128)(2,1)}) %all-gather.24.cloned.1.call-update) | async-done | bytes 2097168 | tf_op jit(solution)/shard_map/all_gather | solution.py:134
  138.0 99.9 %while.27 = (s32[]{:T(128)}, bf16[2,512,4,64]{1,3,2,0:T(8,128)(2,1)}, f32[2,4,512]{2,1,0:T(4,128)S(1)}, s32[2,512]{1,0:T(2,128)S(1)}, s32[4096]{0:T(1024)S(1)}, ...) while((s32[]{:T(128)}, ...), condition=%wide.region_6.7_spmd, body=%wide.region_2.6_spmd.sunk | while | flops 2271357440 | bytes 113924704 | solution.py:73
  140.3 15.8 fusion.181
  156.2 15.6 fusion.182
  171.8 16.2 fusion.183
  190.3 15.8 fusion.181
  206.1 15.6 fusion.182
  221.7 16.2 fusion.183
  244.4 4.3 all_gather.58
  248.8 4.5 all_gather.59
  253.3 94.7 %all-gather.26.cloned.1.call-done = f32[4096,1024]{1,0:T(8,128)} async-done(((f32[1024,1024]{1,0:T(8,128)}), f32[4096,1024]{1,0:T(8,128)}) %all-gather.26.cloned.1.call-update) | async-done | bytes 16777232 | tf_op jit(solution)/shard_map/all_gather | solution.py:36
  348.0 10.4 reduce_sum.171
  363.8 18.7 %all-gather.18.cloned.1.call-done = bf16[1024,1024]{1,0:T(8,128)(2,1)} async-done(((bf16[512,1024]{1,0:T(8,128)(2,1)}), bf16[1024,1024]{1,0:T(8,128)(2,1)}) %all-gather.18.cloned.1.call-update) | async-done | bytes 2097168 | tf_op jit(solution)/shard_map/all_gather | solution.py:113
  382.5 15.5 multiply_convert_fusion.1
  398.0 19.1 %all-gather.20.cloned.1.call-done = bf16[1024,1024]{1,0:T(8,128)(2,1)} async-done(((bf16[1024,512]{1,0:T(8,128)(2,1)}), bf16[1024,1024]{1,0:T(8,128)(2,1)}) %all-gather.20.cloned.1.call-update) | async-done | bytes 2097168 | tf_op jit(solution)/shard_map/all_gather | solution.py:114
  417.1 6.5 fusion.135
  424.1 105.6 %all-gather.28.cloned.1.call-done = f32[4096,1024]{1,0:T(8,128)} async-done(((f32[1024,1024]{1,0:T(8,128)}), f32[4096,1024]{1,0:T(8,128)}) %all-gather.28.cloned.1.call-update) | async-done | bytes 16777232 | tf_op jit(solution)/shard_map/all_gather | solution.py:36
  529.7 10.3 reduce_sum.177
  540.0 4.2 fusion.127
  548.5 3.2 fusion.126
  551.6 3.1 copy-done.41
  554.7 3.9 add_convert_fusion.1
  560.0 4.3 fusion.136
  564.4 106.0 %all-gather.30.cloned.1.call-done = f32[4096,1024]{1,0:T(8,128)} async-done(((f32[1024,1024]{1,0:T(8,128)}), f32[4096,1024]{1,0:T(8,128)}) %all-gather.30.cloned.1.call-update) | async-done | bytes 16777232 | tf_op jit(solution)/shard_map/all_gather | solution.py:36
  670.4 10.3 reduce_sum.186
  680.7 6.4 multiply_reduce_fusion.1
  696.8 338.4 %while.28 = (s32[]{:T(128)}, f32[4096,4,64]{0,2,1:T(8,128)}, f32[4096,4,64]{0,2,1:T(8,128)}, bf16[2,512,4,64]{1,3,2,0:T(8,128)(2,1)}, bf16[2,512,4,64]{1,3,2,0:T...) while((s32[]{:T(128)}, f32[4096,4,64]{0,2,1:T(8,128)}, ...), condition=%wide.region_20.21_spmd.clone, body=%wide.region_18.20_spmd.clone.sunk | while | flops 5595217920 | bytes 414817440 | solution.py:104
  697.0 2.8 compare_and_fusion.3
  699.9 13.1 fusion.196
  713.0 13.1 fusion.195
  726.1 62.6 %fusion.197 = f32[4096,4,64]{0,2,1:T(8,128)} fusion(f32[4,512,4096]{2,1,0:T(8,128)} %fusion.195, f32[4,512,4096]{2,1,0:T(8,128)} %fusion.196, f32[4,512]{1,0:T(4,128)S(1)} %dynamic-slice_bitcast_fusion.2, pred[512,4096]{1,0:T(8,128)(4,1)} %compare_and_fusion.3, f32[4096,4,64]{0,2,1:T(8,128)} %get-tuple-element.498, pred[]{:T(512)S(6)} %compare.3, ...), kind=kOutput, calls=%fused_computation.48.clone.1 | convolution fusion | flops 1168119808 | bytes 147079680 | tf_op jit(solution)/shard_map/while/body/eval_jaxpr/hqk,qhd->khd/dot_general | solution.py:96
  788.7 59.2 %fusion.199 = bf16[2,512,4,64]{1,3,2,0:T(8,128)(2,1)} fusion(bf16[2,512,4,64]{1,3,2,0:T(8,128)(2,1)} %get-tuple-element.500, s32[]{:T(128)} %get-tuple-element.497, bf16[4096,4,64]{0,2,1:T(8,128)(2,1)S(1)} %get-tuple-element.517, f32[4,512,4096]{2,1,0:T(8,128)} %fusion.195, f32[4,512,4096]{2,1,0:T(8,128)} %fusion.196, ...), kind=kOutput, calls=%fused_computation.52.clone.1 | convolution fusion | flops 1166022656 | bytes 141050368 | tf_op jit(solution)/shard_map/while/body/eval_jaxpr/hqk,khd->qhd/dot_general | solution.py:93
  848.0 17.3 fusion.198
  865.3 2.8 compare_and_fusion.3
  868.1 13.1 fusion.196
  881.3 13.1 fusion.195
  894.4 62.9 %fusion.197 = f32[4096,4,64]{0,2,1:T(8,128)} fusion(f32[4,512,4096]{2,1,0:T(8,128)} %fusion.195, f32[4,512,4096]{2,1,0:T(8,128)} %fusion.196, f32[4,512]{1,0:T(4,128)S(1)} %dynamic-slice_bitcast_fusion.2, pred[512,4096]{1,0:T(8,128)(4,1)} %compare_and_fusion.3, f32[4096,4,64]{0,2,1:T(8,128)} %get-tuple-element.498, pred[]{:T(512)S(6)} %compare.3, ...), kind=kOutput, calls=%fused_computation.48.clone.1 | convolution fusion | flops 1168119808 | bytes 147079680 | tf_op jit(solution)/shard_map/while/body/eval_jaxpr/hqk,qhd->khd/dot_general | solution.py:96
  957.3 59.2 %fusion.199 = bf16[2,512,4,64]{1,3,2,0:T(8,128)(2,1)} fusion(bf16[2,512,4,64]{1,3,2,0:T(8,128)(2,1)} %get-tuple-element.500, s32[]{:T(128)} %get-tuple-element.497, bf16[4096,4,64]{0,2,1:T(8,128)(2,1)S(1)} %get-tuple-element.517, f32[4,512,4096]{2,1,0:T(8,128)} %fusion.195, f32[4,512,4096]{2,1,0:T(8,128)} %fusion.196, ...), kind=kOutput, calls=%fused_computation.52.clone.1 | convolution fusion | flops 1166022656 | bytes 141050368 | tf_op jit(solution)/shard_map/while/body/eval_jaxpr/hqk,khd->qhd/dot_general | solution.py:93
  1016.6 18.5 %fusion.198 = f32[4096,4,64]{0,2,1:T(8,128)} fusion(f32[4,512,4096]{2,1,0:T(8,128)} %fusion.196, f32[4,512]{1,0:T(4,128)S(1)} %dynamic-slice_bitcast_fusion.2, pred[512,4096]{1,0:T(8,128)(4,1)} %compare_and_fusion.3, f32[4096,4,64]{0,2,1:T(8,128)} %get-tuple-element.499, pred[]{:T(512)S(6)} %compare.3, ...), kind=kOutput, calls=%fused_computation.50.clone.1 | convolution fusion | flops 1109393408 | bytes 44310532 | tf_op jit(solution)/shard_map/while/body/eval_jaxpr/hqk,qhd->khd/dot_general | solution.py:99
  1035.2 5.7 copy.61
  1041.0 5.6 copy.60
  1048.7 6.6 fusion.118
  1057.0 6.7 fusion.121
  1064.8 3.9 fusion.120
  1072.0 45.9 %reduce-scatter.15.cloned.1.call-done = f32[1024,256]{1,0:T(8,128)} async-done(((f32[4096,256]{1,0:T(8,128)}), f32[1024,256]{1,0:T(8,128)}) %reduce-scatter.15.cloned.1.call-update) | async-done | bytes 1048592 | tf_op jit(solution)/shard_map/reduce_scatter | solution.py:184
  1119.1 78.3 %reduce-scatter.13.cloned.1.call-done = f32[1024,256]{1,0:T(8,128)} async-done(((f32[4096,256]{1,0:T(8,128)}), f32[1024,256]{1,0:T(8,128)}) %reduce-scatter.13.cloned.1.call-update) | async-done | bytes 1048592 | tf_op jit(solution)/shard_map/reduce_scatter | solution.py:181
  1199.5 4.6 fusion.105
  1206.5 48.1 %reduce-scatter.23.cloned.1.call-done = f32[1024,512]{1,0:T(8,128)} async-done(((f32[1024,1024]{1,0:T(8,128)}), f32[1024,512]{1,0:T(8,128)}) %reduce-scatter.23.cloned.1.call-update) | async-done | bytes 2097168 | tf_op jit(solution)/shard_map/reduce_scatter | solution.py:204
  1254.5 56.6 %reduce-scatter.21.cloned.1.call-done = f32[512,1024]{1,0:T(8,128)} async-done(((f32[1024,1024]{1,0:T(8,128)}), f32[512,1024]{1,0:T(8,128)}) %reduce-scatter.21.cloned.1.call-update) | async-done | bytes 2097168 | tf_op jit(solution)/shard_map/reduce_scatter | solution.py:203
  1311.1 23.2 %reduce-scatter.19.cloned.1.call-done = f32[256,512]{1,0:T(8,128)} async-done(((f32[256,1024]{1,0:T(8,128)}), f32[256,512]{1,0:T(8,128)}) %reduce-scatter.19.cloned.1.call-update) | async-done | bytes 524304 | tf_op jit(solution)/shard_map/reduce_scatter | solution.py:202
  1334.3 45.6 %reduce-scatter.17.cloned.1.call-done = f32[3,512,256]{1,2,0:T(8,128)} async-done(((f32[3,1024,256]{1,2,0:T(8,128)}), f32[3,512,256]{1,2,0:T(8,128)}) %reduce-scatter.17.cloned.1.call-update) | async-done | bytes 1572880 | tf_op jit(solution)/shard_map/reduce_scatter | solution.py:201
  1379.9 5.2 convolution_bitcast_fusion
  1385.1 12.0 reduce-scatter.25.cloned.1.call-done
  1398.2 16.3 reduce-scatter.27.cloned.1.call-done
  1415.5 12.8 all-reduce
  1428.4 212.6 %all-reduce.4.cloned.1.call-done = (f32[3,512,256]{1,2,0:T(8,128)}, f32[256,512]{1,0:T(8,128)}, f32[512,1024]{1,0:T(8,128)}, f32[1024,512]{1,0:T(8,128)}) async-done(((f32[3,512,256]{1,2,0:T(8,128)}, f32[256,512]{1,0:T(8,128)}, f32[512,1024]{1,0:T(8,128)}, f32[1024,512]{1,0:T(8,128)}), (f32[3,512,256]{1,2,0:T(8,128)}, f32[256,512]{1,0:T(8,128)}, f32[512,1024]{1,0:T(8,128)}, ...) | async-done | bytes 6291472 | tf_op jit(solution)/shard_map/psum | solution.py:208
  1640.9 3.0 copy.65
  1644.0 103.2 %all-gather.32.cloned.1.call-done = f32[4096,1024]{1,0:T(8,128)} async-done(((f32[1024,1024]{1,0:T(8,128)}), f32[4096,1024]{1,0:T(8,128)}) %all-gather.32.cloned.1.call-update) | async-done | bytes 16777232 | tf_op jit(solution)/shard_map/all_gather | solution.py:36
  1747.2 10.3 reduce_sum.217
  1757.5 5.3 add_convert_fusion
  (194 shorter events, 56.4 us)
Async XLA Ops:
  7.2 32.9 %all-gather.16.cloned.1.call-start = ((), (), s32[]{:S(2)}) async-start(), calls=%async_computation.8 | async-start | bytes 2359296 | tf_op jit(solution)/shard_map/all_gather | solution.py:111
  9.5 81.6 %all-gather.22.cloned.1.call-start = ((), (), s32[]{:S(2)}) async-start(), calls=%async_computation.17 | async-start | bytes 2621440 | tf_op jit(solution)/shard_map/all_gather | solution.py:133
  44.0 1.9 copy-start.39
  44.0 2.3 copy-start.18
  45.1 92.9 %all-gather.24.cloned.1.call-start = ((), (), s32[]{:S(2)}) async-start(), calls=%async_computation.18 | async-start | bytes 2621440 | tf_op jit(solution)/shard_map/all_gather | solution.py:134
  45.8 302.2 %all-gather.26.cloned.1.call-start = ((), (), s32[]{:S(2)}) async-start(), calls=%async_computation.19 | async-start | bytes 20971520 | tf_op jit(solution)/shard_map/all_gather | solution.py:36
  138.0 102.4 %copy-start.11 = (bf16[256,1024]{1,0:T(8,128)(2,1)S(1)}, bf16[256,1024]{1,0:T(8,128)(2,1)}, u32[]{:S(2)}) copy-start(bf16[256,1024]{1,0:T(8,128)(2,1)} %all_gather.55) | copy-start | bytes 1572868
  239.6 0.8 copy-start.7
  243.2 1.2 copy-start.35
  243.2 5.6 copy-start.36
  243.2 139.3 %all-gather.18.cloned.1.call-start = ((), (), s32[]{:S(2)}) async-start(), calls=%async_computation.9 | async-start | bytes 3145728 | tf_op jit(solution)/shard_map/all_gather | solution.py:113
  243.8 173.3 %all-gather.20.cloned.1.call-start = ((), (), s32[]{:S(2)}) async-start(), calls=%async_computation.10 | async-start | bytes 3145728 | tf_op jit(solution)/shard_map/all_gather | solution.py:114
  244.4 285.3 %all-gather.28.cloned.1.call-start = ((), (), s32[]{:S(2)}) async-start(), calls=%async_computation.20 | async-start | bytes 20971520 | tf_op jit(solution)/shard_map/all_gather | solution.py:36
  248.8 438.4 %copy-start.23 = (f32[1,1024]{1,0:T(1,128)}, f32[1,1024]{1,0:T(1,128)S(1)}, u32[]{:S(2)}) copy-start(f32[1,1024]{1,0:T(1,128)S(1)} %get-tuple-element.329) | copy-start | bytes 12292
  253.3 286.7 %copy-start.31 = (f32[1,1024]{1,0:T(1,128)}, f32[1,1024]{1,0:T(1,128)S(1)}, u32[]{:S(2)}) copy-start(f32[1,1024]{1,0:T(1,128)S(1)} %get-tuple-element.331) | copy-start | bytes 12292
  348.0 10.4 copy-start.9
  361.2 2.0 copy-start
  361.2 325.9 %copy-start.19 = (f32[1024]{0:T(1024)}, f32[1024]{0:T(1024)S(1)}, u32[]{:S(2)}) copy-start(f32[1024]{0:T(1024)S(1)} %broadcast_multiply_fusion.1) | copy-start | bytes 12292
  363.8 323.4 %copy-start.21 = (f32[1024]{0:T(1024)}, f32[1024]{0:T(1024)S(1)}, u32[]{:S(2)}) copy-start(f32[1024]{0:T(1024)S(1)} %fusion.114) | copy-start | bytes 12292
  423.6 246.8 %all-gather.30.cloned.1.call-start = ((), (), s32[]{:S(2)}) async-start(), calls=%async_computation.21 | async-start | bytes 20971520 | tf_op jit(solution)/shard_map/all_gather | solution.py:36
  544.3 1.6 copy-start.6
  548.4 3.2 copy-start.38
  548.4 3.2 copy-start.40
  548.5 6.3 copy-start.41
  551.6 7.0 copy-start.5
  551.6 129.1 %copy-start.27 = (f32[1024]{0:T(1024)}, f32[1024]{0:T(1024)S(1)}, u32[]{:S(2)}) copy-start(f32[1024]{0:T(1024)S(1)} %negate_multiply_fusion.2) | copy-start | bytes 12292
  554.7 5.2 copy-start.37
  558.7 1.3 copy-start.43
  564.3 553.5 %reduce-scatter.15.cloned.1.call-start = ((), (), s32[]{:S(2)}) async-start(), calls=%async_computation.12 | async-start | bytes 5242880 | tf_op jit(solution)/shard_map/reduce_scatter | solution.py:184
  680.7 6.4 copy-start.1
  688.9 2.0 copy-start.4
  688.9 7.9 copy-start.25
  690.9 5.9 copy-start.2
  699.8 13.1 copy-start.3
  868.1 13.1 copy-start.3
  1040.9 156.5 %reduce-scatter.13.cloned.1.call-start = ((), (), s32[]{:S(2)}) async-start(), calls=%async_computation.11 | async-start | bytes 5242880 | tf_op jit(solution)/shard_map/reduce_scatter | solution.py:181
  1046.6 0.7 copy-start.28
  1046.6 2.1 copy-start.42
  1046.6 207.9 %reduce-scatter.23.cloned.1.call-start = ((), (), s32[]{:S(2)}) async-start(), calls=%async_computation.16 | async-start | bytes 6291456 | tf_op jit(solution)/shard_map/reduce_scatter | solution.py:204
  1055.3 0.7 copy-start.20
  1055.3 0.7 copy-start.22
  1055.3 0.7 copy-start.24
  1055.3 0.7 copy-start.32
  1055.3 1.6 copy-start.44
  1055.4 255.7 %reduce-scatter.21.cloned.1.call-start = ((), (), s32[]{:S(2)}) async-start(), calls=%async_computation.15 | async-start | bytes 6291456 | tf_op jit(solution)/shard_map/reduce_scatter | solution.py:203
  1063.7 1.0 copy-start.8
  1063.7 1.0 copy-start.26
  1063.7 270.5 %reduce-scatter.19.cloned.1.call-start = ((), (), s32[]{:S(2)}) async-start(), calls=%async_computation.14 | async-start | bytes 1572864 | tf_op jit(solution)/shard_map/reduce_scatter | solution.py:202
  1068.7 130.8 %copy-start.10 = (bf16[1024,1024]{1,0:T(8,128)(2,1)S(1)}, bf16[1024,1024]{1,0:T(8,128)(2,1)}, u32[]{:S(2)}) copy-start(bf16[1024,1024]{1,0:T(8,128)(2,1)} %param.13) | copy-start | bytes 6291460
  1068.7 311.1 %reduce-scatter.17.cloned.1.call-start = ((), (), s32[]{:S(2)}) async-start(), calls=%async_computation.13 | async-start | bytes 4718592 | tf_op jit(solution)/shard_map/reduce_scatter | solution.py:201
  1198.7 0.8 copy-start.15
  1199.5 4.7 copy-start.30
  1199.5 4.7 copy-start.34
  1204.1 1.2 copy-start.29
  1204.1 1.3 copy-start.33
  1204.1 193.0 %reduce-scatter.25.cloned.1.call-start = ((), (), s32[]{:S(2)}) async-start(), calls=%async_computation.23 | async-start | bytes 786432
  1204.2 175.7 %copy-start.14 = (bf16[1,1024,256]{2,1,0:T(8,128)(2,1)S(1)}, bf16[1,1024,256]{2,1,0:T(8,128)(2,1)}, u32[]{:S(2)}) copy-start(bf16[1,1024,256]{2,1,0:T(8,128)(2,1)} %reshape.362) | copy-start | bytes 1572868
  1204.2 175.7 %copy-start.16 = (bf16[1,1024,256]{2,1,0:T(8,128)(2,1)S(1)}, bf16[1,1024,256]{2,1,0:T(8,128)(2,1)}, u32[]{:S(2)}) copy-start(bf16[1,1024,256]{2,1,0:T(8,128)(2,1)} %copy-done.15) | copy-start | bytes 1572868
  1205.3 209.2 %reduce-scatter.27.cloned.1.call-start = ((), (), s32[]{:S(2)}) async-start(), calls=%async_computation.24 | async-start | bytes 786432
  1206.4 434.5 %all-reduce.4.cloned.1.call-start = ((), (), s32[]{:S(2)}) async-start(), calls=%async_computation.25 | async-start | bytes 12582912 | tf_op jit(solution)/shard_map/psum | solution.py:208
  1379.9 367.3 %all-gather.32.cloned.1.call-start = ((), (), s32[]{:S(2)}) async-start(), calls=%async_computation.22 | async-start | bytes 20971520 | tf_op jit(solution)/shard_map/all_gather | solution.py:36
  1757.5 5.4 copy-start.17
  1757.5 6.1 copy-start.13
  1762.9 2.1 copy-start.12
Sparse Core Ops, SparseCore 0:
  10.1 29.8 all-gather.15
  45.2 45.9 all-gather.21
  93.3 44.6 all-gather.23
  243.3 104.6 all-gather.25
  349.4 33.1 all-gather.17
  383.9 33.1 all-gather.19
  423.7 105.9 all-gather.27
  564.5 105.9 all-gather.29
  1041.1 76.7 reduce-scatter.14
  1120.1 77.2 reduce-scatter.12
  1199.7 54.7 reduce-scatter.22
  1256.8 54.3 reduce-scatter.20
  1313.9 20.3 reduce-scatter.18
  1336.5 43.3 reduce-scatter.16
  1382.5 14.5 reduce-scatter.24
  1399.9 14.5 reduce-scatter.26
  1416.9 223.9 all-reduce.3
  1642.4 104.7 all-gather.31
